TPU v7x, 32 devices: a whole 2x2x4 slice. The times are simulated.
32 devices in a mesh: row: 8 (over y, x, core), col: 4 (over z).
Axes of the slice: x: 2, y: 2, z: 4, core: 2. Of those that a mesh axis runs over, the one named last changes fastest.
Arguments:
- left_act: bfloat16 [32, 64, 256], P(None, 'col', 'row'), may hold values from -6 to 6
- right_act: bfloat16 [32, 64, 256], P(None, 'row', 'col'), may hold values from -6 to 6
- cotangent: bfloat16 [256, 256, 128], P('row', 'col'), may hold values from -4 to 4
- weight: bfloat16 [1024, 128], replicated, may hold values from -0.1875 to 0.1875
Outputs:
- grad_left: float32 [32, 64, 256], P(None, 'col', 'row')
- grad_right: float32 [32, 64, 256], P(None, 'row', 'col')
- grad_weight: float32 [1024, 128], P('row')
All inputs are finite; a program needn't handle non-finite values.
Results may differ from a plain program's by a relative error of at most 0.0029.
Values may be sent and summed in bfloat16 or wider, within the bound.
No kernel may reach another device: no remote copies, remote signals or barrier semaphores. Data moves between devices by JAX's collectives and lax.ppermute only.
A program may use at most 128 MiB of HBM per device.

v0:
```python
import jax
import jax.numpy as jnp
from jax import lax
from jax.sharding import PartitionSpec as P

S = 64


def body(left_act, right_act, cotangent, weight):
    left = lax.all_gather(left_act, "col", axis=1, tiled=True)
    right = lax.all_gather(right_act, "row", axis=1, tiled=True)
    first, second = (cotangent.shape[0], cotangent.shape[1])
    chans = left.shape[0]
    outer = (
        jnp.einsum("csi,dsj->ijcd", left, right, preferred_element_type=jnp.float32) / S
    ).astype(jnp.bfloat16)
    outer_flat = outer.reshape(first * second, chans * chans)
    grad_flat = cotangent.reshape(first * second, cotangent.shape[2])
    contract = (((0,), (0,)), ((), ()))
    partial_w = lax.dot_general(outer_flat, grad_flat, contract, preferred_element_type=jnp.float32)
    own_rows = lax.psum_scatter(partial_w, "row", scatter_dimension=0, tiled=True)
    grad_weight = lax.psum(own_rows, "col")
    grad_outer = lax.dot_general(
        grad_flat, weight, (((1,), (1,)), ((), ())), preferred_element_type=jnp.float32
    )
    grad_outer = grad_outer.astype(jnp.bfloat16).reshape(first, second, chans, chans)
    left_part = (
        jnp.einsum("ijcd,dsj->csi", grad_outer, right, preferred_element_type=jnp.float32) / S
    )
    right_part = (
        jnp.einsum("ijcd,csi->dsj", grad_outer, left, preferred_element_type=jnp.float32) / S
    )
    grad_left = lax.psum_scatter(left_part, "col", scatter_dimension=1, tiled=True)
    grad_right = lax.psum_scatter(right_part, "row", scatter_dimension=1, tiled=True)
    return (grad_left, grad_right, grad_weight)


def solution(mesh):
    return jax.shard_map(
        body,
        mesh=mesh,
        in_specs=(P(None, "col", "row"), P(None, "row", "col"), P("row", "col", None), P()),
        out_specs=(P(None, "col", "row"), P(None, "row", "col"), P("row", None)),
        check_vma=False,
    )
```

profile of v0, /device:TPU:0, one launch (start us, length us, event | category | flops | bytes accessed | tf_op | source)
XLA Modules:
  0.0 213.5 jit_solution(4263041880610660756)
XLA Ops:
  7.2 0.0 reduce-scatter.8.cloned.1.call-start
  7.2 17.7 %all_gather.7 = bf16[32,64,32]{2,1,0:T(8,128)(2,1)S(1)} all-gather(bf16[32,16,32]{2,1,0:T(8,128)(2,1)} %param.4), channel_id=1, replica_groups=mesh['row'=8,'col'=4] {'col'}, dimensions={1}, use_global_device_ids=true | all-gather | bytes 163840 | tf_op jit(solution)/shard_map/all_gather | solution.py:10
  24.9 10.3 %all_gather.6 = bf16[32,64,64]{2,1,0:T(8,128)(2,1)S(1)} all-gather(bf16[32,8,64]{2,1,0:T(8,128)(2,1)} %param.5), channel_id=1, replica_groups=mesh['row'=8,'col'=4] {'row'}, dimensions={1}, use_global_device_ids=true | all-gather | bytes 294912 | tf_op jit(solution)/shard_map/all_gather | solution.py:11
  35.2 5.6 %fusion = bf16[32,64,32,32]{1,0,2,3:T(8,128)(2,1)} fusion(bf16[32,64,64]{2,1,0:T(8,128)(2,1)S(1)} %all_gather.6, bf16[32,64,32]{2,1,0:T(8,128)(2,1)S(1)} %all_gather.7), kind=kOutput, calls=%fused_computation.1 | convolution fusion | flops 272629760 | bytes 4587520 | tf_op jit(solution)/shard_map/csi,dsj->ijcd/dot_general | solution.py:15
  40.8 9.1 %copy.20 = bf16[32,64,32,32]{1,0,3,2:T(8,128)(2,1)} copy(bf16[32,64,32,32]{1,0,2,3:T(8,128)(2,1)} %fusion) | data formatting | bytes 8388608 | tf_op jit(solution)/shard_map/convert_element_type | solution.py:16
  49.9 12.4 %reshape.17 = bf16[2048,1024]{0,1:T(8,128)(2,1)} reshape(bf16[32,64,32,32]{1,0,3,2:T(8,128)(2,1)} %copy.20) | data formatting | bytes 8388608 | tf_op jit(solution)/shard_map/reshape | solution.py:17
  62.3 4.3 %fusion.9 = f32[1024,128]{1,0:T(8,128)} fusion(bf16[2048,1024]{0,1:T(8,128)(2,1)} %reshape.17, bf16[2048,128]{1,0:T(8,128)(2,1)S(1)} %bitcast.47), kind=kOutput, calls=%fused_computation.13 | convolution fusion | flops 536870912 | bytes 5242880 | tf_op jit(solution)/shard_map/dot_general | solution.py:20
  66.6 0.0 reduce-scatter.4.cloned.1.call-start
  66.7 3.2 %convolution_convert_fusion = bf16[2048,1024]{1,0:T(8,128)(2,1)} fusion(bf16[2048,128]{1,0:T(8,128)(2,1)S(1)} %bitcast.46, bf16[1024,128]{1,0:T(8,128)(2,1)S(1)} %copy-done.1), kind=kOutput, calls=%fused_computation.2 | convolution fusion | flops 538968064 | bytes 4980736 | tf_op jit(solution)/shard_map/dot_general | solution.py:23
  69.8 6.5 %copy.17 = bf16[2048,1024]{0,1:T(8,128)(2,1)} copy(bf16[2048,1024]{1,0:T(8,128)(2,1)} %convolution_convert_fusion) | data formatting | bytes 8388608 | tf_op jit(solution)/shard_map/convert_element_type | solution.py:26
  76.3 12.9 %reshape.16 = bf16[32,64,32,32]{1,0,3,2:T(8,128)(2,1)} reshape(bf16[2048,1024]{0,1:T(8,128)(2,1)} %copy.17) | data formatting | bytes 8388608 | tf_op jit(solution)/shard_map/reshape | solution.py:26
  89.2 5.7 %fusion.4 = f32[32,64,32]{1,2,0:T(8,128)S(1)} fusion(bf16[32,64,32,32]{1,0,3,2:T(8,128)(2,1)} %reshape.16, bf16[32,64,64]{2,1,0:T(8,128)(2,1)S(1)} %all_gather.6), kind=kOutput, calls=%fused_computation.8 | convolution fusion | flops 268500992 | bytes 4718592 | tf_op jit(solution)/shard_map/ijcd,dsj->csi/dot_general | solution.py:28
  95.0 1.8 copy.18
  96.8 0.2 reduce-scatter.6.cloned.1.call-start
  97.1 7.0 %fusion.2 = f32[32,64,64]{1,2,0:T(8,128)S(1)} fusion(bf16[32,64,32,32]{1,0,3,2:T(8,128)(2,1)} %reshape.16, bf16[32,64,32]{2,1,0:T(8,128)(2,1)S(1)} %all_gather.7), kind=kOutput, calls=%fused_computation.5 | convolution fusion | flops 268566528 | bytes 4849664 | tf_op jit(solution)/shard_map/ijcd,csi->dsj/dot_general | solution.py:31
  104.1 1.8 copy.19
  105.9 0.0 all-reduce.2.cloned.1.call-start
  106.0 0.5 all-reduce.2.cloned.1.call-update
  106.5 24.8 %reduce-scatter.4.cloned.1.call-done = f32[32,16,32]{2,0,1:T(8,128)} async-done(((f32[32,64,32]{2,0,1:T(8,128)}), f32[32,16,32]{2,0,1:T(8,128)}) %reduce-scatter.4.cloned.1.call-update) | async-done | bytes 65552 | tf_op jit(solution)/shard_map/reduce_scatter | solution.py:33
  131.3 1.8 copy.21
  133.1 35.9 %reduce-scatter.6.cloned.1.call-done = f32[32,8,64]{2,0,1:T(8,128)} async-done(((f32[32,64,64]{2,0,1:T(8,128)}), f32[32,8,64]{2,0,1:T(8,128)}) %reduce-scatter.6.cloned.1.call-update) | async-done | bytes 65552 | tf_op jit(solution)/shard_map/reduce_scatter | solution.py:34
  169.0 1.6 copy.22
  170.6 34.9 %all-reduce.2.cloned.1.call-done = f32[128,128]{1,0:T(8,128)} async-done(((f32[128,128]{1,0:T(8,128)}), f32[128,128]{1,0:T(8,128)}) %all-reduce.2.cloned.1.call-update) | async-done | bytes 65552 | tf_op jit(solution)/shard_map/psum | solution.py:22
  205.5 1.5 copy.27
  (8 shorter events, 0.1 us)
Async XLA Ops:
  7.2 55.2 %copy-start = (bf16[32,64,128]{2,1,0:T(8,128)(2,1)S(1)}, bf16[32,64,128]{2,1,0:T(8,128)(2,1)}, u32[]{:S(2)}) copy-start(bf16[32,64,128]{2,1,0:T(8,128)(2,1)} %param.6) | copy-start | bytes 1572868
  7.2 98.8 %reduce-scatter.8.cloned.1.call-start = ((), (), s32[]{:S(2)}) async-start(), calls=%async_computation.5 | async-start | bytes 589824 | tf_op jit(solution)/shard_map/reduce_scatter | solution.py:21
  49.9 16.7 %copy-start.1 = (bf16[1024,128]{1,0:T(8,128)(2,1)S(1)}, bf16[1024,128]{1,0:T(8,128)(2,1)}, u32[]{:S(2)}) copy-start(bf16[1024,128]{1,0:T(8,128)(2,1)} %param.7) | copy-start | bytes 786436
  66.6 64.7 %reduce-scatter.4.cloned.1.call-start = ((), (), s32[]{:S(2)}) async-start(), calls=%async_computation.3 | async-start | bytes 1310720 | tf_op jit(solution)/shard_map/reduce_scatter | solution.py:33
  96.8 72.1 %reduce-scatter.6.cloned.1.call-start = ((), (), s32[]{:S(2)}) async-start(), calls=%async_computation.4 | async-start | bytes 1179648 | tf_op jit(solution)/shard_map/reduce_scatter | solution.py:34
  105.9 99.6 %all-reduce.2.cloned.1.call-start = ((), (), s32[]{:S(2)}) async-start(), calls=%async_computation.6 | async-start | bytes 131072 | tf_op jit(solution)/shard_map/psum | solution.py:22
Sparse Core Ops, SparseCore 0:
  66.7 34.8 reduce-scatter.7
  103.9 27.3 reduce-scatter.3
  134.5 34.4 reduce-scatter.5
  171.1 34.2 all-reduce.1
where the time goes:
time: 215 us; the launch traced here: 213 us
  waiting for transfers between devices  96.1 us (45%)
  local copies, waits for them, and re-layouts  49.4 us (23%)
  blocking collectives  28 us (13%)
  matrix products  25.8 us (12%)
  between operations  13.8 us (6%)
    reduce_scatter x1, waiting for transfers between devices, body(): lax.psum_scatter(right_part, 'row', scatter_dimension=1, tiled=True)  35.9 us
    psum x1, waiting for transfers between devices, body(): grad_weight = lax.psum(own_rows, 'col')  34.9 us
    reduce_scatter x1, waiting for transfers between devices, body(): lax.psum_scatter(left_part, 'col', scatter_dimension=1, tiled=True)  24.8 us
    all_gather x1, blocking collectives, body(): left = lax.all_gather(left_act, 'col', axis=1, tiled=True)  17.7 us
    reshape x1, local copies, waits for them, and re-layouts, body(): grad_outer.astype(jnp.bfloat16).reshape(first, second, chans, chans)  12.9 us
    reshape x1, local copies, waits for them, and re-layouts, body(): outer_flat = outer.reshape(first * second, chans * chans)  12.4 us
    all_gather x1, blocking collectives, body(): right = lax.all_gather(right_act, 'row', axis=1, tiled=True)  10.3 us
    convert_element_type x1, local copies, waits for them, and re-layouts, body(): outer = (jnp.einsum('csi,dsj->ijcd', left, right, preferred_element_type=...  9.13 us
  transfers between devices with their start and end apart: 4, of which 3 were waited for; matrix products, arithmetic and copies ran while one was open for 20% of the time, Pallas kernels for 0%

commit v1 on v0

--- a/solution.py
+++ b/solution.py
@@ -6,8 +6,20 @@
 S = 64
 
 
+def create_turns_in(mine):
+    return jnp.concatenate(
+        lax.all_to_all(
+            jnp.stack(lax.axis_size("col") * [mine], 0),
+            axis_name="col",
+            split_axis=0,
+            concat_axis=0,
+        ),
+        1,
+    )
+
+
 def body(left_act, right_act, cotangent, weight):
-    left = lax.all_gather(left_act, "col", axis=1, tiled=True)
+    left = create_turns_in(left_act)
     right = lax.all_gather(right_act, "row", axis=1, tiled=True)
     first, second = (cotangent.shape[0], cotangent.shape[1])
     chans = left.shape[0]

time: 215 us -> 205 us (0.953)
  blocking collectives: 28 us -> 10.3 us
  starting transfers between devices: 0.34 us -> 6.65 us
  local copies, waits for them, and re-layouts: 49.4 us -> 51.9 us
    all_gather x1 -> x0, blocking collectives: 17.7 us -> none  [body(): left = lax.all_gather(left_act, 'col', axis=1, tiled=True)]
    all_to_all x0 -> x1, starting transfers between devices: none -> 6.35 us  [create_turns_in(): lax.all_to_all(jnp.stack(lax.axis_size('col') * [mine], 0), axis_name='co...]
    unnamed x7 -> x9, local copies, waits for them, and re-layouts: 4.93 us -> 6.36 us
  transfers between devices with their start and end apart: 4 -> 5, of which waited for: 3 -> 3; matrix products, arithmetic and copies ran while one was open for 20% -> 21% of each run, Pallas kernels for 0% -> 0%
where the time goes in v1:
time: 205 us; the launch traced here: 204 us
  waiting for transfers between devices  95.8 us (47%)
  local copies, waits for them, and re-layouts  51.9 us (25%)
  matrix products  25.8 us (13%)
  between operations  13.8 us (7%)
  blocking collectives  10.3 us (5%)
  starting transfers between devices  6.65 us (3%)
    reduce_scatter x1, waiting for transfers between devices, body(): lax.psum_scatter(right_part, 'row', scatter_dimension=1, tiled=True)  35.9 us
    psum x1, waiting for transfers between devices, body(): grad_weight = lax.psum(own_rows, 'col')  34.8 us
    reduce_scatter x1, waiting for transfers between devices, body(): lax.psum_scatter(left_part, 'col', scatter_dimension=1, tiled=True)  24.5 us
    reshape x1, local copies, waits for them, and re-layouts, body(): grad_outer.astype(jnp.bfloat16).reshape(first, second, chans, chans)  12.9 us
    reshape x1, local copies, waits for them, and re-layouts, body(): outer_flat = outer.reshape(first * second, chans * chans)  12.4 us
    all_gather x1, blocking collectives, body(): right = lax.all_gather(right_act, 'row', axis=1, tiled=True)  10.3 us
    convert_element_type x1, local copies, waits for them, and re-layouts, body(): outer = (jnp.einsum('csi,dsj->ijcd', left, right, preferred_element_type=...  9.12 us
    dot_general x1, matrix products, body(): jnp.einsum('ijcd,csi->dsj', grad_outer, left, preferred_element_type=jnp....  7.02 us
  transfers between devices with their start and end apart: 5, of which 3 were waited for; matrix products, arithmetic and copies ran while one was open for 21% of the time, Pallas kernels for 0%

profile of v1, /device:TPU:0, one launch (start us, length us, event | category | flops | bytes accessed | tf_op | source)
XLA Modules:
  0.0 204.3 jit_solution(16011743856938152748)
XLA Ops:
  7.2 1.0 stack.2
  8.2 1.2 reshape.33
  9.4 6.3 %all-to-all-start = ((bf16[4,2,8192]{2,1,0:T(2,128)(2,1)}), bf16[4,2,8192]{2,1,0:T(2,128)(2,1)S(1)}, u32[]{:S(2)}, u32[]{:S(2)}) async-start(bf16[4,2,8192]{2,1,0:T(2,128)(2,1)} %reshape.33), calls=%async_computation.1 | async-start | bytes 262144 | tf_op jit(solution)/shard_map/all_to_all | solution.py:11
  15.7 10.3 %all_gather.3 = bf16[32,64,64]{2,1,0:T(8,128)(2,1)S(1)} all-gather(bf16[32,8,64]{2,1,0:T(8,128)(2,1)} %param.5), channel_id=1, replica_groups=mesh['row'=8,'col'=4] {'row'}, dimensions={1}, use_global_device_ids=true | all-gather | bytes 294912 | tf_op jit(solution)/shard_map/all_gather | solution.py:23
  26.0 0.3 reshape.34
  26.3 5.6 %fusion = bf16[32,64,32,32]{1,0,2,3:T(8,128)(2,1)} fusion(bf16[32,64,32,1]{2,1,0,3:T(8,128)(2,1)S(1)} %bitcast.50, bf16[32,64,64]{2,1,0:T(8,128)(2,1)S(1)} %all_gather.3), kind=kOutput, calls=%fused_computation.1 | convolution fusion | flops 272629760 | bytes 4587520 | tf_op jit(solution)/shard_map/csi,dsj->ijcd/dot_general | solution.py:27
  31.9 9.1 %copy.26 = bf16[32,64,32,32]{1,0,3,2:T(8,128)(2,1)} copy(bf16[32,64,32,32]{1,0,2,3:T(8,128)(2,1)} %fusion) | data formatting | bytes 8388608 | tf_op jit(solution)/shard_map/convert_element_type | solution.py:28
  41.0 12.4 %reshape.27 = bf16[2048,1024]{0,1:T(8,128)(2,1)} reshape(bf16[32,64,32,32]{1,0,3,2:T(8,128)(2,1)} %copy.26) | data formatting | bytes 8388608 | tf_op jit(solution)/shard_map/reshape | solution.py:29
  53.4 4.2 %fusion.7 = f32[1024,128]{1,0:T(8,128)} fusion(bf16[2048,1024]{0,1:T(8,128)(2,1)} %reshape.27, bf16[2048,128]{1,0:T(8,128)(2,1)S(1)} %bitcast.49), kind=kOutput, calls=%fused_computation.11 | convolution fusion | flops 536870912 | bytes 5242880 | tf_op jit(solution)/shard_map/dot_general | solution.py:32
  57.7 0.2 reduce-scatter.4.cloned.1.call-start
  57.9 3.2 %convolution_convert_fusion = bf16[2048,1024]{1,0:T(8,128)(2,1)} fusion(bf16[2048,128]{1,0:T(8,128)(2,1)S(1)} %bitcast.48, bf16[1024,128]{1,0:T(8,128)(2,1)S(1)} %copy-done.1), kind=kOutput, calls=%fused_computation.2 | convolution fusion | flops 538968064 | bytes 4980736 | tf_op jit(solution)/shard_map/dot_general | solution.py:35
  61.1 6.5 %copy.20 = bf16[2048,1024]{0,1:T(8,128)(2,1)} copy(bf16[2048,1024]{1,0:T(8,128)(2,1)} %convolution_convert_fusion) | data formatting | bytes 8388608 | tf_op jit(solution)/shard_map/convert_element_type | solution.py:38
  67.6 12.9 %reshape.24 = bf16[32,64,32,32]{1,0,3,2:T(8,128)(2,1)} reshape(bf16[2048,1024]{0,1:T(8,128)(2,1)} %copy.20) | data formatting | bytes 8388608 | tf_op jit(solution)/shard_map/reshape | solution.py:38
  80.5 5.7 %fusion.4 = f32[32,64,32]{1,2,0:T(8,128)S(1)} fusion(bf16[32,64,32,32]{1,0,3,2:T(8,128)(2,1)} %reshape.24, bf16[32,64,64]{2,1,0:T(8,128)(2,1)S(1)} %all_gather.3), kind=kOutput, calls=%fused_computation.8 | convolution fusion | flops 268500992 | bytes 4718592 | tf_op jit(solution)/shard_map/ijcd,dsj->csi/dot_general | solution.py:40
  86.3 1.8 copy.21
  88.2 7.0 %fusion.2 = f32[32,64,64]{1,2,0:T(8,128)S(1)} fusion(bf16[32,64,32,32]{1,0,3,2:T(8,128)(2,1)} %reshape.24, bf16[32,64,32,1]{2,1,3,0:T(8,128)(2,1)S(1)} %bitcast.51), kind=kOutput, calls=%fused_computation.5 | convolution fusion | flops 268566528 | bytes 4849664 | tf_op jit(solution)/shard_map/ijcd,csi->dsj/dot_general | solution.py:43
  95.2 1.7 copy.24
  97.1 0.5 all-reduce.2.cloned.1.call-update
  97.6 24.5 %reduce-scatter.4.cloned.1.call-done = f32[32,16,32]{2,0,1:T(8,128)} async-done(((f32[32,64,32]{2,0,1:T(8,128)}), f32[32,16,32]{2,0,1:T(8,128)}) %reduce-scatter.4.cloned.1.call-update) | async-done | bytes 65552 | tf_op jit(solution)/shard_map/reduce_scatter | solution.py:45
  122.1 1.8 copy.27
  123.9 35.9 %reduce-scatter.6.cloned.1.call-done = f32[32,8,64]{2,0,1:T(8,128)} async-done(((f32[32,64,64]{2,0,1:T(8,128)}), f32[32,8,64]{2,0,1:T(8,128)}) %reduce-scatter.6.cloned.1.call-update) | async-done | bytes 65552 | tf_op jit(solution)/shard_map/reduce_scatter | solution.py:46
  159.8 1.6 copy.28
  161.4 34.8 %all-reduce.2.cloned.1.call-done = f32[128,128]{1,0:T(8,128)} async-done(((f32[128,128]{1,0:T(8,128)}), f32[128,128]{1,0:T(8,128)}) %all-reduce.2.cloned.1.call-update) | async-done | bytes 65552 | tf_op jit(solution)/shard_map/psum | solution.py:34
  196.3 1.5 copy.37
  (13 shorter events, 0.2 us)
Async XLA Ops:
  7.2 46.3 %copy-start = (bf16[32,64,128]{2,1,0:T(8,128)(2,1)S(1)}, bf16[32,64,128]{2,1,0:T(8,128)(2,1)}, u32[]{:S(2)}) copy-start(bf16[32,64,128]{2,1,0:T(8,128)(2,1)} %param.6) | copy-start | bytes 1572868
  9.4 16.6 %all-to-all-start = ((bf16[4,2,8192]{2,1,0:T(2,128)(2,1)}), bf16[4,2,8192]{2,1,0:T(2,128)(2,1)S(1)}, u32[]{:S(2)}, u32[]{:S(2)}) async-start(bf16[4,2,8192]{2,1,0:T(2,128)(2,1)} %reshape.33), calls=%async_computation.1 | async-start | bytes 262144 | tf_op jit(solution)/shard_map/all_to_all | solution.py:11
  15.7 81.3 %reduce-scatter.8.cloned.1.call-start = ((), (), s32[]{:S(2)}) async-start(), calls=%async_computation.6 | async-start | bytes 589824 | tf_op jit(solution)/shard_map/reduce_scatter | solution.py:33
  41.0 16.9 %copy-start.1 = (bf16[1024,128]{1,0:T(8,128)(2,1)S(1)}, bf16[1024,128]{1,0:T(8,128)(2,1)}, u32[]{:S(2)}) copy-start(bf16[1024,128]{1,0:T(8,128)(2,1)} %param.7) | copy-start | bytes 786436
  57.7 64.4 %reduce-scatter.4.cloned.1.call-start = ((), (), s32[]{:S(2)}) async-start(), calls=%async_computation.4 | async-start | bytes 1310720 | tf_op jit(solution)/shard_map/reduce_scatter | solution.py:45
  88.1 71.7 %reduce-scatter.6.cloned.1.call-start = ((), (), s32[]{:S(2)}) async-start(), calls=%async_computation.5 | async-start | bytes 1179648 | tf_op jit(solution)/shard_map/reduce_scatter | solution.py:46
  97.0 99.3 %all-reduce.2.cloned.1.call-start = ((), (), s32[]{:S(2)}) async-start(), calls=%async_computation.7 | async-start | bytes 131072 | tf_op jit(solution)/shard_map/psum | solution.py:34
Sparse Core Ops, SparseCore 0:
  57.8 34.6 reduce-scatter.7
  94.8 27.2 reduce-scatter.3
  125.3 34.4 reduce-scatter.5
  162.0 34.2 all-reduce.1
